TPU v7x, 128 devices: a whole 4x4x4 slice. The times are simulated.
128 devices in a mesh: nodes: 16 (over x_hi, y, core), feat: 8 (over x_lo, z).
Axes of the slice: x: 4 (x_hi: 2, x_lo: 2; x = x_hi * 2 + x_lo), y: 4, z: 4, core: 2. Of those that a mesh axis runs over, the one named last changes fastest.
Arguments:
- feats: bfloat16 [131072, 128], P('nodes', 'feat'), may hold values from -6 to 6
- tiles: bfloat16 [16, 16, 32, 128, 128], P('nodes'), may hold values from -0.25 to 0.25
- dst_block: int32 [16, 16, 32], P('nodes'), may hold values from 0 to 63
- src_block: int32 [16, 16, 32], P('nodes'), may hold values from 0 to 63
- tile_counts: int32 [16, 16], P('nodes'), may hold values from 1 to 32, as said below
- norm: float32 [131072], P('nodes'), may hold values from 0.3 to 3
- weight: bfloat16 [128, 256], P('feat'), may hold values from -0.5 to 0.5
- bias: float32 [256], P('feat'), may hold values from -3 to 3
- cotangent: bfloat16 [131072, 256], P('nodes', 'feat'), may hold values from -6 to 6
Outputs:
- hidden: bfloat16 [131072, 256], P('nodes', 'feat')
- grad_weight: float32 [128, 256], P('feat')
- grad_bias: float32 [256], P('feat')
- grad_feats: float32 [131072, 128], P('nodes', 'feat')
Inputs may be any that keep to these rules, and one draw needn't show every extreme that they name: Slots at or past tile_counts[o, p] hold no tile; one source slab has 32 tiles from every owner slab in every draw.
All inputs are finite; a program needn't handle non-finite values.
Results may differ from a plain program's by a relative error of at most 0.0075.
Values may be sent and summed in bfloat16 or wider, within the bound.
No kernel may reach another device: no remote copies, remote signals or barrier semaphores. Data moves between devices by JAX's collectives and lax.ppermute only.
A program may use at most 128 MiB of HBM per device.

v0:
```python
import jax
import jax.numpy as jnp
from jax import lax
from jax.sharding import PartitionSpec as P


def silu_slope(pre):
    sigma = jax.nn.sigmoid(pre)
    return sigma * (1.0 + pre * (1.0 - sigma))


def on_device(feats, tiles, dst_block, src_block, tile_counts, norm, weight, bias, cotangent):
    highest = lax.Precision.HIGHEST
    rows_dev = feats.shape[0]
    tile_size = tiles.shape[-1]
    block_count = rows_dev // tile_size
    slot_count = tiles.shape[2]
    feat_local = feats.shape[1]
    own_tiles = tiles[0]
    own_dst = dst_block[0]
    own_src = src_block[0]
    own_counts = tile_counts[0]
    block_ids = jnp.arange(block_count, dtype=jnp.int32)
    slot_ids = jnp.arange(slot_count, dtype=jnp.int32)
    usable_slots = (slot_ids[None, :] < own_counts[:, None]).astype(jnp.float32)
    scaled = (norm[:, None] * feats.astype(jnp.float32)).astype(jnp.bfloat16)
    start_sum = jnp.zeros((block_count, tile_size, feat_local), jnp.float32)
    piece = lax.all_gather(scaled, "nodes", axis=0, tiled=True)
    shards = piece.reshape(piece.shape[0] // rows_dev, block_count, tile_size, feat_local)

    def add_one(position, inner):
        shard = lax.dynamic_index_in_dim(shards, position, 0, keepdims=False)
        tile_set = lax.dynamic_index_in_dim(own_tiles, position, 0, keepdims=False)
        sources = lax.dynamic_index_in_dim(own_src, position, 0, keepdims=False)
        targets = lax.dynamic_index_in_dim(own_dst, position, 0, keepdims=False)
        usable = lax.dynamic_index_in_dim(usable_slots, position, 0, keepdims=False)
        picked = shard[sources]
        product = jnp.einsum("cij,cjf->cif", tile_set, picked, preferred_element_type=jnp.float32)
        placing = (targets[:, None] == block_ids[None, :]).astype(jnp.float32) * usable[:, None]
        return inner + jnp.einsum("cb,cif->bif", placing, product, precision=highest)

    summed = lax.fori_loop(0, shards.shape[0], add_one, start_sum)
    aggregated = (norm[:, None] * summed.reshape(rows_dev, feat_local)).astype(jnp.bfloat16)
    partial_pre = jnp.dot(aggregated, weight, preferred_element_type=jnp.float32)
    pre = lax.psum_scatter(partial_pre, "feat", scatter_dimension=1, tiled=True) + bias
    hidden = jax.nn.silu(pre).astype(jnp.bfloat16)
    grad_pre = (cotangent.astype(jnp.float32) * silu_slope(pre)).astype(jnp.bfloat16)
    piece = lax.all_gather(grad_pre, "feat", axis=1, tiled=True)
    projected = lax.dot_general(
        piece, weight, (((1,), (1,)), ((), ())), preferred_element_type=jnp.float32
    )
    block = lax.dot_general(
        aggregated, piece, (((0,), (0,)), ((), ())), preferred_element_type=jnp.float32
    )
    projected, weight_part = (projected, block)
    scale = (rows_dev * lax.axis_size("nodes")) ** (-0.5)
    bias_part = jnp.sum(grad_pre, axis=0, dtype=jnp.float32)
    weight_sum, bias_sum = lax.psum((weight_part, bias_part), "nodes")
    grad_weight = weight_sum * scale
    grad_bias = bias_sum * scale
    back_scaled = (norm[:, None] * projected).astype(jnp.bfloat16)
    back_blocks = back_scaled.reshape(block_count, tile_size, feat_local)
    picked_back = back_blocks[own_dst]
    partial_back = (
        jnp.einsum("pcij,pcif->pcjf", own_tiles, picked_back, preferred_element_type=jnp.float32)
        * usable_slots[:, :, None, None]
    )
    sources = own_src
    placing = (sources[..., None] == block_ids).astype(jnp.float32)
    returned = lax.psum_scatter(
        jnp.einsum("pcb,pcjf->pbjf", placing, partial_back, precision=highest).reshape(
            rows_dev * lax.axis_size("nodes"), feat_local
        ),
        "nodes",
        scatter_dimension=0,
        tiled=True,
    )
    grad_feats = norm[:, None] * returned
    return (hidden, grad_weight, grad_bias, grad_feats)


def solution(mesh):
    return jax.shard_map(
        on_device,
        mesh=mesh,
        in_specs=(
            P("nodes", "feat"),
            P("nodes", None, None, None, None),
            P("nodes", None, None),
            P("nodes", None, None),
            P("nodes", None),
            P("nodes"),
            P("feat", None),
            P("feat"),
            P("nodes", "feat"),
        ),
        out_specs=(P("nodes", "feat"), P("feat", None), P("feat"), P("nodes", "feat")),
        check_vma=False,
    )
```

profile of v0, /device:TPU:0, one launch (start us, length us, event | category | flops | bytes accessed | tf_op | source)
XLA Modules:
  0.0 432.4 jit_solution(2135381942234439921)
XLA Ops:
  9.7 59.0 %all-gather.3.cloned.1.call-done = bf16[131072,16]{0,1:T(8,128)(2,1)} async-done(((bf16[8192,16]{0,1:T(8,128)(2,1)}), bf16[131072,16]{0,1:T(8,128)(2,1)}) %all-gather.3.cloned.1.call-update) | async-done | bytes 4194320 | tf_op jit(solution)/shard_map/all_gather | solution.py:28
  68.8 4.9 %copy.24 = bf16[2,8,1024,128]{3,2,1,0:T(8,128)(2,1)} copy(bf16[2,8,1024,128]{3,1,2,0:T(8,128)(2,1)} %bitcast.97) | data formatting | bytes 8388608
  73.7 72.4 %while.14 = (s32[]{:T(128)}, f32[64,128,16]{1,0,2:T(8,128)S(1)}, s32[16,32]{1,0:T(8,128)S(1)}, f32[16,32]{1,0:T(8,128)S(1)}, bf16[16,32,128,128]{3,2,1,0:T(8,128...) while((s32[]{:T(128)}, f32[64,128,16]{1,0,2:T(8,128)S(1)}, ...), condition=%wide.region_1.2_spmd.clone, body=%wide.region_0.1_spmd.clone.sunk | while | flops 67376224 | bytes 4068739 | solution.py:42
  75.6 1.9 fusion.54
  80.1 1.9 fusion.54
  84.6 1.9 fusion.54
  89.1 1.9 fusion.54
  93.7 1.9 fusion.54
  98.2 1.9 fusion.54
  102.7 1.9 fusion.54
  107.2 1.9 fusion.54
  111.8 1.9 fusion.54
  116.3 1.9 fusion.54
  120.8 1.9 fusion.54
  125.4 1.9 fusion.54
  129.9 1.9 fusion.54
  134.4 1.9 fusion.54
  138.9 1.9 fusion.54
  143.5 1.9 fusion.54
  146.2 4.5 %fusion.28 = f32[8192,256]{0,1:T(8,128)} fusion(bf16[16,256]{1,0:T(8,128)(2,1)S(1)} %copy-done, f32[2,8,64,128]{3,2,1,0:T(8,128)S(1)} %bitcast.94, f32[8192]{0:T(1024)S(1)} %copy-done.2), kind=kOutput, calls=%fused_computation.48 | convolution fusion | flops 67371008 | bytes 8953856 | tf_op jit(solution)/shard_map/dot_general | solution.py:44
  150.7 90.9 %reduce-scatter.3.cloned.1.call-done = f32[8192,32]{0,1:T(8,128)} async-done(((f32[8192,256]{0,1:T(8,128)}), f32[8192,32]{0,1:T(8,128)}) %reduce-scatter.3.cloned.1.call-update) | async-done | bytes 1048592 | tf_op jit(solution)/shard_map/reduce_scatter | solution.py:45
  241.6 2.9 convert_reduce_fusion
  244.7 51.5 %all-gather.5.cloned.1.call-done = bf16[8192,256]{0,1:T(8,128)(2,1)} async-done(((bf16[8192,32]{0,1:T(8,128)(2,1)}), bf16[8192,256]{0,1:T(8,128)(2,1)}) %all-gather.5.cloned.1.call-update) | async-done | bytes 4194320 | tf_op jit(solution)/shard_map/all_gather | solution.py:48
  296.2 2.8 fusion.21
  299.1 2.0 gather_fusion.1
  301.1 8.4 %fusion.31 = f32[16,32,16,128]{3,2,1,0:T(8,128)S(1)} fusion(bf16[16,32,128,16]{2,3,1,0:T(8,128)(2,1)S(1)} %bitcast.88, bf16[1,16,32,128,128]{4,3,2,1,0:T(8,128)(2,1)} %bitcast.91), kind=kOutput, calls=%fused_computation.55 | convolution fusion | flops 268435456 | bytes 23068672 | tf_op jit(solution)/shard_map/pcij,pcif->pcjf/dot_general | solution.py:65
  309.6 5.0 %fusion.18 = f32[16,64,128,16]{2,1,0,3:T(8,128)S(1)} fusion(s32[16,32]{1,0:T(8,128)S(1)} %get-tuple-element.291, f32[16,32,16,128]{3,2,1,0:T(8,128)S(1)} %fusion.31, f32[16,32]{1,0:T(8,128)S(1)} %get-tuple-element.290), kind=kOutput, calls=%fused_computation.30 | convolution fusion | flops 806387712 | bytes 12587008 | tf_op jit(solution)/shard_map/pcb,pcjf->pbjf/dot_general | solution.py:71
  314.6 8.1 %copy.43 = f32[2,8,1024,128]{3,1,2,0:T(8,128)} copy(f32[2,8,1024,128]{3,2,1,0:T(8,128)S(1)} %bitcast.93) | data formatting | bytes 16777216
  322.7 3.4 fusion.26
  326.1 69.7 %all-reduce = (f32[16,256]{1,0:T(8,128)S(1)}, f32[32]{0:T(128)S(1)}) all-reduce(f32[16,256]{1,0:T(8,128)S(1)} %fusion.26, f32[32]{0:T(128)S(1)} %get-tuple-element.200), channel_id=1, replica_groups=mesh['nodes'=16,'feat'=8] {'nodes'}, use_global_device_ids=true, to_apply=%region_3.4 | all-reduce | flops 4128 | bytes 33024 | tf_op jit(solution)/shard_map/psum | solution.py:58
  397.0 27.0 %reduce-scatter.5.cloned.1.call-done = f32[8192,16]{0,1:T(8,128)} async-done(((f32[131072,16]{0,1:T(8,128)}), f32[8192,16]{0,1:T(8,128)}) %reduce-scatter.5.cloned.1.call-update) | async-done | bytes 524304 | tf_op jit(solution)/shard_map/reduce_scatter | solution.py:70
  424.0 1.9 broadcast_multiply_fusion
  (159 shorter events, 45.5 us)
Async XLA Ops:
  7.2 139.0 %copy-start = (bf16[16,256]{1,0:T(8,128)(2,1)S(1)}, bf16[16,256]{1,0:T(8,128)(2,1)}, u32[]{:S(2)}) copy-start(bf16[16,256]{1,0:T(8,128)(2,1)} %param.17) | copy-start | bytes 24580
  7.2 61.6 %all-gather.3.cloned.1.call-start = ((), (), s32[]{:S(2)}) async-start(), calls=%async_computation.2 | async-start | bytes 4456448 | tf_op jit(solution)/shard_map/all_gather | solution.py:28
  9.0 232.7 %reduce-scatter.3.cloned.1.call-start = ((), (), s32[]{:S(2)}) async-start(), calls=%async_computation.3 | async-start | bytes 9437184 | tf_op jit(solution)/shard_map/reduce_scatter | solution.py:45
  68.8 4.9 %copy-start.4 = (s32[1,16,32]{2,1,0:T(8,128)S(1)}, s32[1,16,32]{2,1,0:T(8,128)}, u32[]{:S(2)}) copy-start(s32[1,16,32]{2,1,0:T(8,128)} %param.14) | copy-start | bytes 6148
  68.8 4.9 %copy-start.5 = (s32[1,16,32]{2,1,0:T(8,128)S(1)}, s32[1,16,32]{2,1,0:T(8,128)}, u32[]{:S(2)}) copy-start(s32[1,16,32]{2,1,0:T(8,128)} %param.13) | copy-start | bytes 6148
  73.7 72.4 %copy-start.2 = (f32[8192]{0:T(1024)S(1)}, f32[8192]{0:T(1024)}, u32[]{:S(2)}) copy-start(f32[8192]{0:T(1024)} %param.16) | copy-start | bytes 98308
  150.7 91.0 %copy-start.3 = (bf16[8192,32]{0,1:T(8,128)(2,1)S(1)}, bf16[8192,32]{0,1:T(8,128)(2,1)}, u32[]{:S(2)}) copy-start(bf16[8192,32]{0,1:T(8,128)(2,1)} %param.19) | copy-start | bytes 1572868
  150.7 91.0 %copy-start.6 = (f32[32]{0:T(128)S(1)}, f32[32]{0:T(128)}, u32[]{:S(2)}) copy-start(f32[32]{0:T(128)} %param.18) | copy-start | bytes 388
  150.7 145.5 %all-gather.5.cloned.1.call-start = ((), (), s32[]{:S(2)}) async-start(), calls=%async_computation.4 | async-start | bytes 4718592 | tf_op jit(solution)/shard_map/all_gather | solution.py:48
  244.5 179.4 %reduce-scatter.5.cloned.1.call-start = ((), (), s32[]{:S(2)}) async-start(), calls=%async_computation.5 | async-start | bytes 8912896 | tf_op jit(solution)/shard_map/reduce_scatter | solution.py:70
  322.7 103.2 %copy-start.1 = (bf16[16,256]{1,0:T(8,128)(2,1)S(1)}, bf16[16,256]{1,0:T(8,128)(2,1)}, u32[]{:S(2)}) copy-start(bf16[16,256]{1,0:T(8,128)(2,1)} %param.17) | copy-start | bytes 24580
Sparse Core Ops, SparseCore 0:
  11.1 57.6 all-gather.2
  150.8 90.7 reduce-scatter.2
  244.7 51.4 all-gather.4
  322.8 101.1 reduce-scatter.4
where the time goes:
time: 434 us; the launch traced here: 432 us
  waiting for transfers between devices  228 us (53%)
  blocking collectives  69.7 us (16%)
  matrix products  67 us (15%)
  local copies, waits for them, and re-layouts  43.6 us (10%)
  between operations  13.9 us (3%)
  other arithmetic  8.6 us (2%)
    reduce_scatter x1, waiting for transfers between devices, on_device(): lax.psum_scatter(partial_pre, 'feat', scatter_dimension=1, tiled=True)  90.9 us
    psum x1, blocking collectives, on_device(): weight_sum, bias_sum = lax.psum((weight_part, bias_part), 'nodes')  69.7 us
    all_gather x1, waiting for transfers between devices, on_device(): piece = lax.all_gather(scaled, 'nodes', axis=0, tiled=True)  59 us
    all_gather x1, waiting for transfers between devices, on_device(): piece = lax.all_gather(grad_pre, 'feat', axis=1, tiled=True)  51.5 us
    dot_general x16, matrix products, add_one(): jnp.einsum('cij,cjf->cif', tile_set, picked, preferred_element_type=jnp.f...  29.8 us
    reduce_scatter x1, waiting for transfers between devices, on_device(): lax.psum_scatter(jnp.einsum('pcb,pcjf->pbjf', placing, partial_back, prec...  27 us
    dynamic_slice x32, local copies, waits for them, and re-layouts, add_one(): shard = lax.dynamic_index_in_dim(shards, position, 0, keepdims=False)  18.5 us
    unnamed x16, local copies, waits for them, and re-layouts  13 us
  transfers between devices with their start and end apart: 4, of which 4 were waited for; matrix products, arithmetic and copies ran while one was open for 1% of the time, Pallas kernels for 0%

commit v1 on v0

--- a/solution.py
+++ b/solution.py
@@ -2,6 +2,13 @@
 import jax.numpy as jnp
 from jax import lax
 from jax.sharding import PartitionSpec as P
+
+
+def exchange_gather(block, axis, d):
+    count = lax.axis_size(axis)
+    tiles = jnp.stack([block for _ in range(count)])
+    tiles = lax.all_to_all(tiles, axis, split_axis=0, concat_axis=0)
+    return jnp.concatenate(tiles, axis=d)
 
 
 def silu_slope(pre):
@@ -25,7 +32,7 @@
     usable_slots = (slot_ids[None, :] < own_counts[:, None]).astype(jnp.float32)
     scaled = (norm[:, None] * feats.astype(jnp.float32)).astype(jnp.bfloat16)
     start_sum = jnp.zeros((block_count, tile_size, feat_local), jnp.float32)
-    piece = lax.all_gather(scaled, "nodes", axis=0, tiled=True)
+    piece = exchange_gather(scaled, "nodes", 0)
     shards = piece.reshape(piece.shape[0] // rows_dev, block_count, tile_size, feat_local)
 
     def add_one(position, inner):

time: 434 us -> 449 us (1.035)
  starting transfers between devices: 0.16 us -> 7.42 us
  waiting for transfers between devices: 228 us -> 235 us
    all_gather x1 -> x0, waiting for transfers between devices: 59 us -> none  [on_device(): piece = lax.all_gather(scaled, 'nodes', axis=0, tiled=True)]
    all_to_all x0 -> x1, waiting for transfers between devices: none -> 55.4 us  [exchange_gather(): tiles = lax.all_to_all(tiles, axis, split_axis=0, concat_axis=0)]
    reduce_scatter x1, waiting for transfers between devices: 90.9 us -> 101 us  [on_device(): lax.psum_scatter(partial_pre, 'feat', scatter_dimension=1, tiled=True)]
    all_to_all x0 -> x1, starting transfers between devices: none -> 7.3 us  [exchange_gather(): tiles = lax.all_to_all(tiles, axis, split_axis=0, concat_axis=0)]
    unnamed x16 -> x18, local copies, waits for them, and re-layouts: 13 us -> 13.5 us
where the time goes in v1:
time: 449 us; the launch traced here: 448 us
  waiting for transfers between devices  235 us (52%)
  blocking collectives  69.7 us (16%)
  matrix products  67 us (15%)
  local copies, waits for them, and re-layouts  46.4 us (10%)
  between operations  13.9 us (3%)
  starting transfers between devices  7.42 us (2%)
  other arithmetic  7.25 us (2%)
    reduce_scatter x1, waiting for transfers between devices, on_device(): lax.psum_scatter(partial_pre, 'feat', scatter_dimension=1, tiled=True)  101 us
    psum x1, blocking collectives, on_device(): weight_sum, bias_sum = lax.psum((weight_part, bias_part), 'nodes')  69.7 us
    all_to_all x1, waiting for transfers between devices, exchange_gather(): tiles = lax.all_to_all(tiles, axis, split_axis=0, concat_axis=0)  55.4 us
    all_gather x1, waiting for transfers between devices, on_device(): piece = lax.all_gather(grad_pre, 'feat', axis=1, tiled=True)  51.5 us
    dot_general x16, matrix products, add_one(): jnp.einsum('cij,cjf->cif', tile_set, picked, preferred_element_type=jnp.f...  29.8 us
    reduce_scatter x1, waiting for transfers between devices, on_device(): lax.psum_scatter(jnp.einsum('pcb,pcjf->pbjf', placing, partial_back, prec...  27 us
    dynamic_slice x32, local copies, waits for them, and re-layouts, add_one(): shard = lax.dynamic_index_in_dim(shards, position, 0, keepdims=False)  18.4 us
    unnamed x18, local copies, waits for them, and re-layouts  13.5 us
  transfers between devices with their start and end apart: 4, of which 4 were waited for; matrix products, arithmetic and copies ran while one was open for 1% of the time, Pallas kernels for 0%

profile of v1, /device:TPU:0, one launch (start us, length us, event | category | flops | bytes accessed | tf_op | source)
XLA Modules:
  0.0 447.6 jit_solution(5569428834225058130)
XLA Ops:
  8.2 2.4 stack.2
  10.6 7.3 %all-to-all-start = ((bf16[16,8192,16]{1,2,0:T(8,128)(2,1)}), bf16[16,8192,16]{1,2,0:T(8,128)(2,1)}, u32[]{:S(2)}, u32[]{:S(2)}) async-start(bf16[16,8192,16]{1,2,0:T(8,128)(2,1)} %stack.2), calls=%async_computation | async-start | bytes 8388608 | tf_op jit(solution)/shard_map/all_to_all | solution.py:10
  18.1 55.4 %all-to-all-done = bf16[16,8192,16]{1,2,0:T(8,128)(2,1)} async-done(((bf16[16,8192,16]{1,2,0:T(8,128)(2,1)}), bf16[16,8192,16]{1,2,0:T(8,128)(2,1)}, u32[]{:S(2)}, u32[]{:S(2)}) %all-to-all-start) | async-done | bytes 4194336 | tf_op jit(solution)/shard_map/all_to_all | solution.py:10
  73.5 5.4 %copy.24 = bf16[32,8,64,128]{3,2,1,0:T(8,128)(2,1)} copy(bf16[32,8,64,128]{3,1,2,0:T(8,128)(2,1)} %bitcast.19) | data formatting | bytes 8388608
  78.8 72.4 %while.14 = (s32[]{:T(128)}, f32[64,128,16]{1,0,2:T(8,128)S(1)}, s32[16,32]{1,0:T(8,128)S(1)}, f32[16,32]{1,0:T(8,128)S(1)}, bf16[16,32,128,128]{3,2,1,0:T(8,128...) while((s32[]{:T(128)}, f32[64,128,16]{1,0,2:T(8,128)S(1)}, ...), condition=%wide.region_1.2_spmd.clone, body=%wide.region_0.1_spmd.clone.sunk | while | flops 67376224 | bytes 4068739 | solution.py:49
  80.7 1.9 fusion.54
  85.2 1.9 fusion.54
  89.7 1.9 fusion.54
  94.2 1.9 fusion.54
  98.8 1.9 fusion.54
  103.3 1.9 fusion.54
  107.8 1.9 fusion.54
  112.3 1.9 fusion.54
  116.9 1.9 fusion.54
  121.4 1.9 fusion.54
  125.9 1.9 fusion.54
  130.4 1.9 fusion.54
  135.0 1.9 fusion.54
  139.5 1.9 fusion.54
  151.2 4.5 %fusion.28 = f32[8192,256]{0,1:T(8,128)} fusion(bf16[16,256]{1,0:T(8,128)(2,1)S(1)} %copy-done, f32[2,8,64,128]{3,2,1,0:T(8,128)S(1)} %bitcast.95, f32[8192]{0:T(1024)S(1)} %copy-done.2), kind=kOutput, calls=%fused_computation.48 | convolution fusion | flops 67371008 | bytes 8953856 | tf_op jit(solution)/shard_map/dot_general | solution.py:51
  155.8 101.0 %reduce-scatter.3.cloned.1.call-done = f32[8192,32]{0,1:T(8,128)} async-done(((f32[8192,256]{0,1:T(8,128)}), f32[8192,32]{0,1:T(8,128)}) %reduce-scatter.3.cloned.1.call-update) | async-done | bytes 1048592 | tf_op jit(solution)/shard_map/reduce_scatter | solution.py:52
  256.8 2.9 convert_reduce_fusion
  259.9 51.5 %all-gather.2.cloned.1.call-done = bf16[8192,256]{0,1:T(8,128)(2,1)} async-done(((bf16[8192,32]{0,1:T(8,128)(2,1)}), bf16[8192,256]{0,1:T(8,128)(2,1)}) %all-gather.2.cloned.1.call-update) | async-done | bytes 4194320 | tf_op jit(solution)/shard_map/all_gather | solution.py:55
  311.4 2.8 fusion.21
  314.3 2.0 gather_fusion.1
  316.3 8.4 %fusion.31 = f32[16,32,16,128]{3,2,1,0:T(8,128)S(1)} fusion(bf16[16,32,128,16]{2,3,1,0:T(8,128)(2,1)S(1)} %bitcast.89, bf16[1,16,32,128,128]{4,3,2,1,0:T(8,128)(2,1)} %bitcast.92), kind=kOutput, calls=%fused_computation.55 | convolution fusion | flops 268435456 | bytes 23068672 | tf_op jit(solution)/shard_map/pcij,pcif->pcjf/dot_general | solution.py:72
  324.8 5.0 %fusion.18 = f32[16,64,128,16]{2,1,0,3:T(8,128)S(1)} fusion(s32[16,32]{1,0:T(8,128)S(1)} %get-tuple-element.282, f32[16,32,16,128]{3,2,1,0:T(8,128)S(1)} %fusion.31, f32[16,32]{1,0:T(8,128)S(1)} %get-tuple-element.281), kind=kOutput, calls=%fused_computation.30 | convolution fusion | flops 806387712 | bytes 12587008 | tf_op jit(solution)/shard_map/pcb,pcjf->pbjf/dot_general | solution.py:78
  329.8 8.1 %copy.43 = f32[2,8,1024,128]{3,1,2,0:T(8,128)} copy(f32[2,8,1024,128]{3,2,1,0:T(8,128)S(1)} %bitcast.94) | data formatting | bytes 16777216
  337.9 3.4 fusion.26
  341.3 69.7 %all-reduce = (f32[16,256]{1,0:T(8,128)S(1)}, f32[32]{0:T(128)S(1)}) all-reduce(f32[16,256]{1,0:T(8,128)S(1)} %fusion.26, f32[32]{0:T(128)S(1)} %get-tuple-element.193), channel_id=1, replica_groups=mesh['nodes'=16,'feat'=8] {'nodes'}, use_global_device_ids=true, to_apply=%region_3.4 | all-reduce | flops 4128 | bytes 33024 | tf_op jit(solution)/shard_map/psum | solution.py:65
  412.2 27.0 %reduce-scatter.5.cloned.1.call-done = f32[8192,16]{0,1:T(8,128)} async-done(((f32[131072,16]{0,1:T(8,128)}), f32[8192,16]{0,1:T(8,128)}) %reduce-scatter.5.cloned.1.call-update) | async-done | bytes 524304 | tf_op jit(solution)/shard_map/reduce_scatter | solution.py:77
  439.1 1.9 broadcast_multiply_fusion
  (161 shorter events, 47.8 us)
Async XLA Ops:
  7.2 144.1 %copy-start = (bf16[16,256]{1,0:T(8,128)(2,1)S(1)}, bf16[16,256]{1,0:T(8,128)(2,1)}, u32[]{:S(2)}) copy-start(bf16[16,256]{1,0:T(8,128)(2,1)} %param.17) | copy-start | bytes 24580
  10.6 7.4 %copy-start.7 = (s32[1,16]{1,0:T(1,128)S(1)}, s32[1,16]{1,0:T(1,128)}, u32[]{:S(2)}) copy-start(s32[1,16]{1,0:T(1,128)} %param.15) | copy-start | bytes 196
  10.6 62.8 %all-to-all-start = ((bf16[16,8192,16]{1,2,0:T(8,128)(2,1)}), bf16[16,8192,16]{1,2,0:T(8,128)(2,1)}, u32[]{:S(2)}, u32[]{:S(2)}) async-start(bf16[16,8192,16]{1,2,0:T(8,128)(2,1)} %stack.2), calls=%async_computation | async-start | bytes 8388608 | tf_op jit(solution)/shard_map/all_to_all | solution.py:10
  17.9 238.9 %reduce-scatter.3.cloned.1.call-start = ((), (), s32[]{:S(2)}) async-start(), calls=%async_computation.3 | async-start | bytes 9437184 | tf_op jit(solution)/shard_map/reduce_scatter | solution.py:52
  73.4 5.4 %copy-start.4 = (s32[1,16,32]{2,1,0:T(8,128)S(1)}, s32[1,16,32]{2,1,0:T(8,128)}, u32[]{:S(2)}) copy-start(s32[1,16,32]{2,1,0:T(8,128)} %param.14) | copy-start | bytes 6148
  73.5 5.4 %copy-start.5 = (s32[1,16,32]{2,1,0:T(8,128)S(1)}, s32[1,16,32]{2,1,0:T(8,128)}, u32[]{:S(2)}) copy-start(s32[1,16,32]{2,1,0:T(8,128)} %param.13) | copy-start | bytes 6148
  78.8 72.4 %copy-start.2 = (f32[8192]{0:T(1024)S(1)}, f32[8192]{0:T(1024)}, u32[]{:S(2)}) copy-start(f32[8192]{0:T(1024)} %param.16) | copy-start | bytes 98308
  155.7 101.1 %copy-start.3 = (bf16[8192,32]{0,1:T(8,128)(2,1)S(1)}, bf16[8192,32]{0,1:T(8,128)(2,1)}, u32[]{:S(2)}) copy-start(bf16[8192,32]{0,1:T(8,128)(2,1)} %param.19) | copy-start | bytes 1572868
  155.7 101.1 %copy-start.6 = (f32[32]{0:T(128)S(1)}, f32[32]{0:T(128)}, u32[]{:S(2)}) copy-start(f32[32]{0:T(128)} %param.18) | copy-start | bytes 388
  155.8 155.6 %all-gather.2.cloned.1.call-start = ((), (), s32[]{:S(2)}) async-start(), calls=%async_computation.4 | async-start | bytes 4718592 | tf_op jit(solution)/shard_map/all_gather | solution.py:55
  259.7 179.4 %reduce-scatter.5.cloned.1.call-start = ((), (), s32[]{:S(2)}) async-start(), calls=%async_computation.5 | async-start | bytes 8912896 | tf_op jit(solution)/shard_map/reduce_scatter | solution.py:77
  337.9 103.1 %copy-start.1 = (bf16[16,256]{1,0:T(8,128)(2,1)S(1)}, bf16[16,256]{1,0:T(8,128)(2,1)}, u32[]{:S(2)}) copy-start(bf16[16,256]{1,0:T(8,128)(2,1)} %param.17) | copy-start | bytes 24580
Sparse Core Ops, SparseCore 0:
  155.9 100.8 reduce-scatter.2
  259.9 51.4 all-gather.1
  338.0 101.0 reduce-scatter.4
